TPU v7x, 1024 devices: a whole 4x8x16 slice. The times are simulated.
1024 devices in a mesh: section: 16 (over z), expert: 64 (over y, x, core).
Axes of the slice: x: 4, y: 8, z: 16, core: 2. Of those that a mesh axis runs over, the one named last changes fastest.
Arguments:
- next_grad: bfloat16 [16, 1024, 3584], P('section', 'expert'), may hold values from -6 to 6
- routes: int32 [16, 1024, 8], P('section', 'expert'), may hold values from 0 to 63, all different within a row; in each aligned block of 16 rows (0 to 15, 16 to 31, ..., all dimensions but the last counted through in order) at most 4 rows name the same one
- gates: float32 [16, 1024, 8], P('section', 'expert'), may hold values from 0.1 to 0.6
- saved: bfloat16 [16, 64, 256, 2048], P('section', 'expert'), may hold values from -5 to 5
- w_down: bfloat16 [64, 1024, 3584], P('expert'), may hold values from -0.1875 to 0.1875
Outputs:
- hidden_grads: bfloat16 [16, 64, 256, 2048], P('section', 'expert')
Inputs may be any that keep to these rules, and one draw needn't show every extreme that they name: `routes`: each row names 8 different experts; among the 16 rows of one device no expert is named by more than 4 rows, and in every draw some expert is named by exactly 4 rows of some device.
All inputs are finite; a program needn't handle non-finite values.
Results may differ from a plain program's by a relative error of at most 0.005.
Values may be sent and summed in bfloat16 or wider, within the bound.
A program may use at most 32 MiB of HBM per device.

v0:
```python
import jax
import jax.numpy as jnp
from jax import lax
from jax.sharding import PartitionSpec as P


def passed_along(x, axis, by):
    peers = lax.axis_size(axis)
    return lax.ppermute(x, axis, [(i, (i + by) % peers) for i in range(peers)])


def assign_table(routes, gates, experts):
    expert_ids = jnp.arange(experts, dtype=jnp.int32)
    match = routes[:, :, None] == expert_ids[None, None, :]
    return jnp.sum(jnp.where(match, gates[:, :, None], 0.0), axis=1)


def build_rows(grad, assign, most):
    live = (assign > 0.0).astype(jnp.int32)
    before = jnp.cumsum(live, axis=0) - live
    places = jnp.arange(most, dtype=jnp.int32)
    pick = (before[:, :, None] == places[None, None, :]) & (live[:, :, None] > 0)
    tok_rows = pick.shape[0]
    token_ids = jnp.arange(tok_rows, dtype=jnp.int32)[:, None, None]
    chosen = jnp.sum(jnp.where(pick, token_ids, 0), axis=0)
    weight = jnp.sum(jnp.where(pick, assign[:, :, None], 0.0), axis=0)
    filled = jnp.any(pick, axis=0)
    flat_ids = chosen.reshape(-1)
    taken = jnp.take(grad, flat_ids, axis=0).astype(jnp.float32)
    scaled = weight.reshape(-1)[:, None] * taken
    rows = jnp.where(filled.reshape(-1)[:, None], scaled, 0.0)
    return rows.astype(jnp.bfloat16).reshape(pick.shape[1], most, grad.shape[1])


def dispatch(rows):
    return lax.all_to_all(rows, "expert", split_axis=0, concat_axis=0, tiled=True)


def per_device(next_grad, routes, gates, saved, w_down):
    experts = lax.axis_size("expert")
    slots = saved.shape[2]
    most = slots // experts
    hidden_width = w_down.shape[1]
    assign = assign_table(routes[0], gates[0], experts)
    grad = passed_along(next_grad[0], "section", -1)
    received = dispatch(build_rows(grad, assign, most))
    received = received.reshape(slots, received.shape[2])
    hidden = lax.dot_general(
        received, w_down[0], (((1,), (1,)), ((), ())), preferred_element_type=jnp.float32
    )
    pre_gate = saved[0, 0, :, :hidden_width].astype(jnp.float32)
    pre_up = saved[0, 0, :, hidden_width:].astype(jnp.float32)
    sig = jax.nn.sigmoid(pre_gate)
    d_up = hidden * pre_gate * sig
    d_gate = hidden * pre_up * sig * (1.0 + pre_gate * (1.0 - sig))
    result = jnp.concatenate([d_gate, d_up], axis=-1).astype(jnp.bfloat16)
    return result[None, None]


def solution(mesh):
    return jax.shard_map(
        per_device,
        mesh=mesh,
        in_specs=(
            P("section", "expert", None),
            P("section", "expert", None),
            P("section", "expert", None),
            P("section", "expert", None, None),
            P("expert", None, None),
        ),
        out_specs=P("section", "expert", None, None),
        check_vma=False,
    )
```

profile of v0, /device:TPU:1, one launch (start us, length us, event | category | flops | bytes accessed | tf_op | source)
XLA Modules:
  0.0 92.7 jit_solution(11701811153843402889)
XLA Ops:
  0.0 18.7 %collective-permute-start = (bf16[16,3584]{1,0:T(8,128)(2,1)}, bf16[16,3584]{1,0:T(8,128)(2,1)S(1)}, u32[]{:S(2)}, u32[]{:S(2)}) collective-permute-start(bf16[16,3584]{1,0:T(8,128)(2,1)} %bitcast.30), channel_id=1, source_target_pairs={{0,960},{64,0},{128,64},{192,128},{256,192},{320,256},{384,320},{4... | collective-permute-start | bytes 344072 | tf_op jit(solution)/shard_map/ppermute | solution.py:9
  18.8 0.8 copy.10
  19.5 0.8 copy.11
  20.3 0.1 select_reduce_fusion
  20.5 0.1 copy.15
  20.6 0.1 reshape.114
  20.8 0.1 copy.14
  20.9 0.1 copy.12
  21.0 0.1 copy.13
  21.1 0.0 collective-permute-done
  21.1 1.7 %gather_fusion = bf16[256,3584]{1,0:T(8,128)(2,1)S(1)} fusion(bf16[16,3584]{1,0:T(8,128)(2,1)S(1)} %collective-permute-done, s32[1024]{0:T(1024)S(1)} %pad_clamp_fusion), kind=kCustom, calls=%fused_computation | custom fusion | bytes 3671040 | tf_op jit(solution)/shard_map/jit(_take)/gather | solution.py:29
  22.8 1.5 %gather.7 = bf16[64,4,3584]{2,1,0:T(4,128)(2,1)} reshape(bf16[256,3584]{1,0:T(8,128)(2,1)S(1)} %gather_fusion) | data formatting | bytes 3670016 | tf_op jit(solution)/shard_map/jit(_take)/gather | solution.py:29
  24.3 4.2 %select_convert_fusion = bf16[64,4,3584]{2,1,0:T(4,128)(2,1)} fusion(bf16[64,4,3584]{2,1,0:T(4,128)(2,1)} %gather.7, f32[64,4]{1,0:T(8,128)S(1)} %copy.13, pred[64,4]{1,0:T(8,128)(4,1)S(1)} %copy.14, pred[64,4]{1,0:T(8,128)(4,1)S(1)} %copy.12), kind=kLoop, calls=%fused_computation.3 | loop fusion | flops 4587520 | bytes 3671552 | tf_op jit(solution)/shard_map/convert_element_type | solution.py:32
  28.5 11.4 %all-to-all-start = ((bf16[64,4,3584]{2,1,0:T(4,128)(2,1)}), bf16[64,4,3584]{2,1,0:T(4,128)(2,1)S(1)}, u32[]{:S(2)}, u32[]{:S(2)}) async-start(bf16[64,4,3584]{2,1,0:T(4,128)(2,1)} %select_convert_fusion), calls=%async_computation | async-start | bytes 3670016 | tf_op jit(solution)/shard_map/all_to_all | solution.py:36
  39.9 0.0 copy-start
  40.0 44.4 %all-to-all-done = bf16[64,4,3584]{2,1,0:T(4,128)(2,1)S(1)} async-done(((bf16[64,4,3584]{2,1,0:T(4,128)(2,1)}), bf16[64,4,3584]{2,1,0:T(4,128)(2,1)S(1)}, u32[]{:S(2)}, u32[]{:S(2)}) %all-to-all-start) | async-done | bytes 1835040 | tf_op jit(solution)/shard_map/all_to_all | solution.py:36
  84.3 1.5 %reshape.115 = bf16[256,3584]{1,0:T(8,128)(2,1)} reshape(bf16[64,4,3584]{2,1,0:T(4,128)(2,1)S(1)} %all-to-all-done) | data formatting | bytes 3670016 | tf_op jit(solution)/shard_map/reshape | solution.py:47
  85.8 0.0 copy-done
  85.8 6.9 %fusion.12 = (bf16[1,1,256,2048]{3,2,1,0:T(8,128)(2,1)}, bf16[1,1,256,2048]{3,2,1,0:T(8,128)(2,1)}) fusion(bf16[1,1,256,2048]{3,2,1,0:T(8,128)(2,1)S(1)} %copy-done, bf16[256,3584]{1,0:T(8,128)(2,1)} %reshape.115, bf16[1,1024,3584]{2,1,0:T(8,128)(2,1)} %param.9, bf16[1,1,256,2048]{3,2,1,0:T(8,128)(2,1)} %custom-call.2), kind=kOutput, output_to_operand_aliasing={{0}: (3, {}), {1}: (3, {})}, calls=%fused_computation.19 | convolution fusion | flops 1882980352 | bytes 11272192 | tf_op jit(solution)/shard_map/dot_general | solution.py:48
  (10 shorter events, 0.2 us)
Async XLA Ops:
  0.0 21.1 %collective-permute-start = (bf16[16,3584]{1,0:T(8,128)(2,1)}, bf16[16,3584]{1,0:T(8,128)(2,1)S(1)}, u32[]{:S(2)}, u32[]{:S(2)}) collective-permute-start(bf16[16,3584]{1,0:T(8,128)(2,1)} %bitcast.30), channel_id=1, source_target_pairs={{0,960},{64,0},{128,64},{192,128},{256,192},{320,256},{384,320},{4... | collective-permute-start | bytes 344072 | tf_op jit(solution)/shard_map/ppermute | solution.py:9
  28.5 55.8 %all-to-all-start = ((bf16[64,4,3584]{2,1,0:T(4,128)(2,1)}), bf16[64,4,3584]{2,1,0:T(4,128)(2,1)S(1)}, u32[]{:S(2)}, u32[]{:S(2)}) async-start(bf16[64,4,3584]{2,1,0:T(4,128)(2,1)} %select_convert_fusion), calls=%async_computation | async-start | bytes 3670016 | tf_op jit(solution)/shard_map/all_to_all | solution.py:36
  39.9 45.9 %copy-start = (bf16[1,1,256,2048]{3,2,1,0:T(8,128)(2,1)S(1)}, bf16[1,1,256,2048]{3,2,1,0:T(8,128)(2,1)}, u32[]{:S(2)}) copy-start(bf16[1,1,256,2048]{3,2,1,0:T(8,128)(2,1)} %param.8) | copy-start | bytes 3145732
where the time goes:
time: 93.3 us; the launch traced here: 92.7 us
  waiting for transfers between devices  44.4 us (48%)
  starting transfers between devices  30.2 us (32%)
  matrix products  6.94 us (7%)
  local copies, waits for them, and re-layouts  6.71 us (7%)
  other arithmetic  4.45 us (5%)
    all_to_all x1, waiting for transfers between devices, dispatch(): lax.all_to_all(rows, 'expert', split_axis=0, concat_axis=0, tiled=True)  44.4 us
    ppermute x1, starting transfers between devices, passed_along(): return lax.ppermute(x, axis, [(i, (i + by) % peers) for i in range(peers)])  18.7 us
    all_to_all x1, starting transfers between devices, dispatch(): lax.all_to_all(rows, 'expert', split_axis=0, concat_axis=0, tiled=True)  11.4 us
    dot_general x1, matrix products, per_device(): lax.dot_general(received, w_down[0], (((1,), (1,)), ((), ())), preferred_...  6.94 us
    convert_element_type x1, other arithmetic, build_rows(): return rows.astype(jnp.bfloat16).reshape(pick.shape[1], most, grad.shape[1])  4.19 us
    gather x2, local copies, waits for them, and re-layouts, build_rows(): taken = jnp.take(grad, flat_ids, axis=0).astype(jnp.float32)  3.2 us
  transfers between devices with their start and end apart: 2, of which 1 were waited for; matrix products, arithmetic and copies ran while one was open for 2% of the time, Pallas kernels for 0%

commit v1 on v0

v1 whole, which is shorter than its diff:
```python
import functools

import jax
import jax.numpy as jnp
from jax import lax
from jax.experimental import pallas as pl
from jax.experimental.pallas import tpu as pltpu
from jax.sharding import PartitionSpec as P

MESH = pl.DeviceIdType.MESH
NX, NY, NCORE = 4, 8, 2
MOST = 4
CW = 512
BF, F32, I32 = jnp.bfloat16, jnp.float32, jnp.int32


def kernel(sections, nc, grad, routes, gates, saved, w_down, out,
           tok, row, snd, wv, sv, gfac, ufac, acc, rts, gts, meta, pick, weight, perm,
           s_y, r_y, s_x, r_x, s_z, r_z, s_r, r_r, l_in, l_w):
    s, e = lax.axis_index("section"), lax.axis_index("expert")
    y, x, c = e // (NX * NCORE), (e // NCORE) % NX, e % NCORE
    toks = grad.shape[0]
    width = w_down.shape[0]
    ncols = width // 4

    def at(ds, dy, dx, core):
        ss = (s + ds + sections) % sections
        yy, xx = (y + dy + NY) % NY, (x + dx + NX) % NX
        return (ss, (yy * NX + xx) * NCORE + core)

    in_copies = [
        pltpu.make_async_copy(routes, rts, l_in.at[0]),
        pltpu.make_async_copy(gates, gts, l_in.at[1]),
        pltpu.make_async_copy(saved, sv, l_in.at[2]),
    ]
    for cp in in_copies:
        cp.start()
    w_copies = [
        pltpu.make_async_copy(w_down.at[:, pl.ds(k * CW, CW)], wv.at[k], l_w.at[k]) for k in range(nc)
    ]
    for cp in w_copies:
        cp.start()

    barrier = pltpu.get_barrier_semaphore()
    peers = [at(0, 0, 0, 1 - c), at(0, 1, 0, c), at(0, -1, 0, c), at(1, 0, 0, c), at(-1, 0, 0, c)]
    peers += [at(0, 0, dx, core) for dx in (1, -1) for core in range(NCORE)]
    for peer in peers:
        pl.semaphore_signal(barrier, inc=1, device_id=peer, device_id_type=MESH)
    in_copies[0].wait()
    in_copies[1].wait()
    meta[0, y, :, 0:toks] = rts[...].astype(F32)
    meta[0, y, :, toks : 2 * toks] = gts[...]
    pl.semaphore_wait(barrier, len(peers))

    sends = []

    def send(src, dst, ssem, rsem, dev):
        cp = pltpu.make_async_remote_copy(
            src_ref=src, dst_ref=dst, send_sem=ssem, recv_sem=rsem, device_id=dev, device_id_type=MESH
        )
        cp.start()
        sends.append(cp)

    def recv(ref, ssem, rsem):
        pltpu.make_async_remote_copy(
            src_ref=ref, dst_ref=ref, send_sem=ssem, recv_sem=rsem, device_id=at(0, 1, 0, c), device_id_type=MESH
        ).wait_recv()

    def shard(k, b, yy):
        if k == nc:
            return meta.at[b, yy]
        return tok.at[k, pl.ds(pl.multiple_of((b * NY + yy) * toks, toks), toks), :]

    def far(b, up):
        return 4 if (b == 0) == up else 3

    def y_send(k, b, up, d):
        step = 1 if up else -1
        ref = shard(k, b, (y - step * d + NY) % NY)
        i = (b * 2 + int(up)) * 4 + d
        send(ref, ref, s_y.at[k, i], r_y.at[k, i], at(0, step, 0, c))

    def y_recv(k, b, up, d):
        step = 1 if up else -1
        i = (b * 2 + int(up)) * 4 + d - 1
        recv(shard(k, b, (y - step * d + NY) % NY), s_y.at[k, i], r_y.at[k, i])

    def first(k):
        if k < nc:
            recv(shard(k, 0, y), s_z.at[k], r_z.at[k])
        send(shard(k, 0, y), shard(k, 1, y), s_x.at[k], r_x.at[k], at(0, 0, 1, c))
        y_send(k, 0, True, 0)
        y_send(k, 0, False, 0)

    def first_b(k):
        recv(shard(k, 1, y), s_x.at[k], r_x.at[k])
        y_send(k, 1, True, 0)
        y_send(k, 1, False, 0)

    def hop(k, b, d):
        for up in (True, False):
            if d <= far(b, up):
                y_recv(k, b, up, d)
                if d < far(b, up):
                    y_send(k, b, up, d)

    targets = [
        [(x, c), (x, 1 - c), ((x - 1 + NX) % NX, 0), ((x - 1 + NX) % NX, 1)],
        [(x, c), (x, 1 - c), ((x + 1) % NX, 0), ((x + 1) % NX, 1)],
    ]

    def build_tables():
        lane = lax.broadcasted_iota(I32, (8, 128), 1)
        group = lane // toks
        tables = []
        for b in range(2):
            named = jnp.zeros((8, 128), F32)
            gate = jnp.zeros((8, 128), F32)
            for j in range(NY):
                m = meta[b, j]
                r = m if j == 0 else pltpu.roll(m, toks * j, 1)
                shift = (toks * j - toks) % 128
                g = m if shift == 0 else pltpu.roll(m, shift, 1)
                named = jnp.where(group == j, r, named)
                gate = jnp.where(group == j, g, gate)
            for xt, ct in targets[b]:
                expert = ((y * NX + xt) * NCORE + ct).astype(F32)
                tables.append(jnp.sum(jnp.where(named == expert, gate, 0.0), axis=0, keepdims=True))
        assign = jnp.concatenate(tables, axis=0)
        live = (assign > 0.0).astype(F32)
        a = lax.broadcasted_iota(I32, (128, 128), 0)
        b_ = lax.broadcasted_iota(I32, (128, 128), 1)
        tri = jnp.where((a // toks == b_ // toks) & (a < b_), 1.0, 0.0).astype(BF)
        before = jnp.dot(live.astype(BF), tri, preferred_element_type=F32)
        before = jnp.where(assign > 0.0, before, -1.0)
        ri = lax.broadcasted_iota(I32, (NY * MOST, 128), 0)
        li = lax.broadcasted_iota(I32, (NY * MOST, 128), 1)
        same = (ri // MOST) == (li // toks)
        place = (ri % MOST).astype(F32)
        for b in range(2):
            for t in range(4):
                i = b * 4 + t
                r0 = i * NY * MOST
                hit = same & (jnp.broadcast_to(before[i : i + 1], ri.shape) == place)
                wt = jnp.sum(jnp.where(hit, jnp.broadcast_to(assign[i : i + 1], ri.shape), 0.0), axis=1, keepdims=True)
                pick[r0 : r0 + NY * MOST, b * 128 : (b + 1) * 128] = jnp.where(hit, 1.0, 0.0).astype(BF)
                pick[r0 : r0 + NY * MOST, (1 - b) * 128 : (2 - b) * 128] = jnp.zeros((NY * MOST, 128), BF)
                weight[r0 : r0 + NY * MOST, :] = jnp.broadcast_to(wt, (NY * MOST, 128))

    def build_perm():
        slot = lax.broadcasted_iota(I32, (256, 256), 0)
        col = lax.broadcasted_iota(I32, (256, 256), 1)
        ys, xs, cs, p = slot // 32, (slot // 8) % NX, (slot // 4) % NCORE, slot % MOST
        dx = (xs - x + NX) % NX
        rel = jnp.where(dx == 0, 0, jnp.where(dx == 3, 1, jnp.where(dx == 1, 2, 3)))
        perm[...] = jnp.where(col == cs * 128 + rel * 32 + ys * 4 + p, 1.0, 0.0).astype(BF)

    def factors(q):
        n = sv.shape[0] // 4
        sl = slice(q * n, (q + 1) * n)
        pre_gate = sv[sl, :width].astype(F32)
        pre_up = sv[sl, width:].astype(F32)
        sig = jax.nn.sigmoid(pre_gate)
        ufac[sl, :] = pre_gate * sig
        gfac[sl, :] = pre_up * sig * (1.0 + pre_gate * (1.0 - sig))

    def select(k):
        n = NY * MOST
        res = jnp.dot(pick[...], tok[k], preferred_element_type=F32)
        wt = weight[...]
        rows = jnp.concatenate([res[:, i * 128 : (i + 1) * 128] * wt for i in range(CW // 128)], axis=1).astype(BF)
        for i, slot in ((1, 0), (5, 1), (2, 2), (3, 3), (6, 4), (7, 5)):
            snd[k, slot] = rows[i * n : (i + 1) * n]
        row[k, c, 0] = rows[0:n]
        row[k, c, 1] = rows[4 * n : 5 * n]
        for core in range(NCORE):
            send(snd.at[k, 2 + core], row.at[k, c, 2], s_r.at[k, 1 + core], r_r.at[k, 1 + c], at(0, 0, -1, core))
            send(snd.at[k, 4 + core], row.at[k, c, 3], s_r.at[k, 3 + core], r_r.at[k, 3 + c], at(0, 0, 1, core))
        send(snd.at[k, 0:2], row.at[k, c, 0:2], s_r.at[k, 0], r_r.at[k, 0], at(0, 0, 0, 1 - c))

    def main(k):
        recv(row.at[k, 1 - c, 0:2], s_r.at[k, 0], r_r.at[k, 0])
        for core in range(NCORE):
            recv(row.at[k, core, 2], s_r.at[k, 1 + core], r_r.at[k, 1 + core])
            recv(row.at[k, core, 3], s_r.at[k, 3 + core], r_r.at[k, 3 + core])
        w_copies[k].wait()
        lhs = jnp.dot(perm[...], row[k].reshape(256, CW), preferred_element_type=F32).astype(BF)
        for n in range(4):
            cols = slice(n * ncols, (n + 1) * ncols)
            part = lax.dot_general(lhs, wv[k, cols, :], (((1,), (1,)), ((), ())), preferred_element_type=F32)
            if k > 0:
                part = acc[:, cols] + part
            if k < nc - 1:
                acc[:, cols] = part
            else:
                ups = slice(width + n * ncols, width + (n + 1) * ncols)
                out[:, cols] = (part * gfac[:, cols]).astype(BF)
                out[:, ups] = (part * ufac[:, cols]).astype(BF)

    for k in range(nc):
        send(grad.at[:, pl.ds(k * CW, CW)], shard(k, 0, y), s_z.at[k], r_z.at[k], at(-1, 0, 0, c))

    order = [nc] + list(range(nc))

    def chunk(i):
        return order[i] if 0 <= i < len(order) else None

    for tick in range(len(order) + 6):
        todo = [
            (lambda k: first(k), 0),
            (lambda k: first_b(k), 1),
            (lambda k: hop(k, 0, 1), 1),
            (lambda k: hop(k, 1, 1), 2),
            (lambda k: hop(k, 0, 2), 2),
            (lambda k: hop(k, 1, 2), 3),
            (lambda k: hop(k, 0, 3), 3),
            (lambda k: hop(k, 1, 3), 4),
            (lambda k: hop(k, 0, 4), 4),
            (lambda k: hop(k, 1, 4), 5),
            (lambda k: build_tables() if k == nc else select(k), 5),
            (lambda k: None if k == nc else main(k), 6),
        ]
        for act, lag in todo:
            k = chunk(tick - lag)
            if k is not None:
                act(k)
        if tick == 0:
            build_perm()
            in_copies[2].wait()
        if tick < 4:
            factors(tick)

    for cp in sends:
        cp.wait_send()


def per_device(sections, next_grad, routes, gates, saved, w_down):
    toks, d = next_grad.shape[1:]
    slots, width2 = saved.shape[2:]
    width = width2 // 2
    nc = d // CW
    dma = pltpu.SemaphoreType.DMA
    res = pl.pallas_call(
        functools.partial(kernel, sections, nc),
        out_shape=jax.ShapeDtypeStruct((slots, width2), BF),
        in_specs=[pl.BlockSpec(memory_space=pltpu.HBM)] * 5,
        out_specs=pl.BlockSpec(memory_space=pltpu.VMEM),
        scratch_shapes=[
            pltpu.VMEM((nc, 2 * NY * toks, CW), BF),
            pltpu.VMEM((nc, NCORE, 4, NY * MOST, CW), BF),
            pltpu.VMEM((nc, 6, NY * MOST, CW), BF),
            pltpu.VMEM((nc, width, CW), BF),
            pltpu.VMEM((slots, width2), BF),
            pltpu.VMEM((slots, width), F32),
            pltpu.VMEM((slots, width), F32),
            pltpu.VMEM((slots, width), F32),
            pltpu.VMEM(routes.shape[:0:-1], I32),
            pltpu.VMEM(gates.shape[:0:-1], F32),
            pltpu.VMEM((2, NY, 8, 128), F32),
            pltpu.VMEM((256, 256), BF),
            pltpu.VMEM((256, 128), F32),
            pltpu.VMEM((256, 256), BF),
            dma((nc + 1, 16)),
            dma((nc + 1, 16)),
            dma((nc + 1,)),
            dma((nc + 1,)),
            dma((nc,)),
            dma((nc,)),
            dma((nc, 5)),
            dma((nc, 5)),
            dma((3,)),
            dma((nc,)),
        ],
        compiler_params=pltpu.CompilerParams(collective_id=0, has_side_effects=True, vmem_limit_bytes=40 << 20),
    )(*[pltpu.with_memory_space_constraint(v, pltpu.HBM) for v in (next_grad[0], routes[0].T, gates[0].T, saved[0, 0], w_down[0])])
    return res[None, None]


def solution(mesh):
    return jax.shard_map(
        functools.partial(per_device, mesh.shape["section"]),
        mesh=mesh,
        in_specs=(
            P("section", "expert", None),
            P("section", "expert", None),
            P("section", "expert", None),
            P("section", "expert", None, None),
            P("expert", None, None),
        ),
        out_specs=P("section", "expert", None, None),
        check_vma=False,
    )
```

time: 93.3 us -> 64.8 us (0.69)
  Pallas kernels: 0 us -> 63.7 us
  waiting for transfers between devices: 44.4 us -> 0 us
  starting transfers between devices: 30.2 us -> 0 us
  matrix products: 6.94 us -> 0 us
  local copies, waits for them, and re-layouts: 6.71 us -> 0.97 us
  other arithmetic: 4.45 us -> 0 us
    pallas_call x0 -> x1, Pallas kernels: none -> 63.7 us  [per_device(): pl.pallas_call(functools.partial(kernel, sections, nc), out_shape=jax.Sha...]
    all_to_all x1 -> x0, waiting for transfers between devices: 44.4 us -> none  [dispatch(): lax.all_to_all(rows, 'expert', split_axis=0, concat_axis=0, tiled=True)]
    ppermute x1 -> x0, starting transfers between devices: 18.7 us -> none  [passed_along(): return lax.ppermute(x, axis, [(i, (i + by) % peers) for i in range(peers)])]
    all_to_all x1 -> x0, starting transfers between devices: 11.4 us -> none  [dispatch(): lax.all_to_all(rows, 'expert', split_axis=0, concat_axis=0, tiled=True)]
    dot_general x1 -> x0, matrix products: 6.94 us -> none  [per_device(): lax.dot_general(received, w_down[0], (((1,), (1,)), ((), ())), preferred_...]
    convert_element_type x1 -> x0, other arithmetic: 4.19 us -> none  [build_rows(): return rows.astype(jnp.bfloat16).reshape(pick.shape[1], most, grad.shape[1])]
    gather x2 -> x0, local copies, waits for them, and re-layouts: 3.2 us -> none  [build_rows(): taken = jnp.take(grad, flat_ids, axis=0).astype(jnp.float32)]
    reshape x2 -> x0, local copies, waits for them, and re-layouts: 1.57 us -> none  [the longest x1 1.46 us: per_device(): received = received.reshape(slots, received.shape[2])]
  transfers between devices with their start and end apart: 2 -> 0, of which waited for: 1 -> 0; matrix products, arithmetic and copies ran while one was open for 2% -> 0% of each run, Pallas kernels for 0% -> 0%
where the time goes in v1:
time: 64.8 us; the launch traced here: 64.7 us
  Pallas kernels  63.7 us (98%)
  local copies, waits for them, and re-layouts  0.97 us (1%)
    pallas_call x1, Pallas kernels, per_device(): pl.pallas_call(functools.partial(kernel, sections, nc), out_shape=jax.Sha...  63.7 us

profile of v1, /device:TPU:1, one launch (start us, length us, event | category | flops | bytes accessed | tf_op | source)
XLA Modules:
  0.0 64.7 jit_solution(7743544856164636775)
XLA Ops:
  0.0 63.7 %shard_map.55 = bf16[256,2048]{1,0:T(8,128)(2,1)S(1)} custom-call(bf16[16,3584]{1,0:T(8,128)(2,1)} %bitcast.13, s32[8,16]{1,0:T(8,128)} %bitcast.14, f32[8,16]{1,0:T(8,128)} %bitcast.15, bf16[256,2048]{1,0:T(8,128)(2,1)} %bitcast.12, bf16[1024,3584]{1,0:T(8,128)(2,1)} %bitcast.11), custom_call_target="tpu_custom_call" | custom-call | tf_op jit(solution)/shard_map/pallas_call | solution.py:243
  63.7 1.0 %copy.7 = bf16[1,1,256,2048]{3,2,1,0:T(8,128)(2,1)} copy(bf16[1,1,256,2048]{3,2,1,0:T(8,128)(2,1)S(1)} %bitcast.10) | data formatting | bytes 2097152

commit v2 on v0

v2 whole, which is shorter than its diff:
```python
import functools

import jax
import jax.numpy as jnp
from jax import lax
from jax.experimental import pallas as pl
from jax.experimental.pallas import tpu as pltpu
from jax.sharding import PartitionSpec as P

MESH = pl.DeviceIdType.MESH
NX, NY, NCORE = 4, 8, 2
MOST = 4
CW = 512
BF, F32, I32 = jnp.bfloat16, jnp.float32, jnp.int32

ORDER = (
    (0, 0, 0, 0), (0, 0, 1, 0), (0, 1, 0, 0), (5, 7, 0, 2), (0, 1, 1, 0), (0, 2, 0, 0), (0, 2, 1, 0), (0, 3, 0, 0),
    (0, 3, 1, 0), (0, 4, 0, 0), (1, 0, 0, 1), (0, 4, 1, 0), (0, 5, 0, 0), (1, 0, 1, 1), (1, 1, 0, 1), (0, 5, 1, 0),
    (0, 6, 0, 0), (1, 1, 1, 1), (1, 2, 0, 1), (1, 2, 1, 1), (5, 7, 0, 3), (1, 3, 0, 1), (1, 3, 1, 1), (1, 4, 0, 1),
    (1, 0, 0, 2), (1, 4, 1, 1), (1, 5, 0, 1), (1, 0, 1, 2), (1, 1, 0, 2), (0, 6, 1, 0), (5, 7, 0, 4), (1, 5, 1, 1),
    (1, 1, 1, 2), (1, 2, 0, 2), (1, 2, 1, 2), (1, 3, 0, 2), (1, 3, 1, 2), (3, 7, 0, 0), (1, 0, 0, 3), (1, 4, 0, 2),
    (1, 4, 1, 2), (1, 6, 0, 1), (1, 0, 1, 3), (1, 5, 0, 2), (1, 1, 0, 3), (1, 6, 1, 1), (1, 5, 1, 2), (1, 1, 1, 3),
    (1, 2, 0, 3), (1, 2, 1, 3), (1, 3, 0, 3), (1, 3, 1, 3), (2, 0, 0, 0), (1, 4, 0, 3), (1, 4, 1, 3), (2, 0, 1, 0),
    (1, 6, 0, 2), (1, 5, 0, 3), (2, 1, 0, 0), (1, 6, 1, 2), (2, 1, 1, 0), (1, 5, 1, 3), (2, 2, 1, 0), (2, 2, 0, 0),
    (2, 3, 1, 0), (3, 0, 0, 0), (2, 3, 0, 0), (2, 4, 0, 0), (2, 4, 1, 0), (1, 6, 0, 3), (2, 5, 0, 0), (3, 1, 0, 0),
    (1, 6, 1, 3), (3, 2, 0, 0), (2, 5, 1, 0), (3, 3, 0, 0), (3, 4, 0, 0), (2, 6, 0, 0), (3, 5, 0, 0), (2, 6, 1, 0),
    (4, 0, 0, 0), (4, 1, 0, 0), (3, 6, 0, 0), (4, 2, 0, 0), (4, 3, 0, 0), (4, 4, 0, 0), (4, 5, 0, 0), (4, 6, 0, 0),
)


def kernel(sections, nc, grad, routes, gates, saved, w_down, out,
           tok, row, snd, wv, sv, gfac, ufac, acc, rts, gts, meta, pick, weight, perm,
           r_y, r_z, r_x, r_d, r_r, r_m, s_tok, l_in, l_w):
    s, e = lax.axis_index("section"), lax.axis_index("expert")
    y, x, c = e // (NX * NCORE), (e // NCORE) % NX, e % NCORE
    toks = grad.shape[0]
    width = w_down.shape[0]
    ncols = width // 4
    n = NY * MOST
    col = NY * toks

    def at(ds, dy, dx, core):
        ss = (s + ds + sections) % sections
        yy, xx = (y + dy + NY) % NY, (x + dx + NX) % NX
        return (ss, (yy * NX + xx) * NCORE + core)

    barrier = pltpu.get_barrier_semaphore()
    peers = [at(0, 0, 0, 1 - c), at(0, 1, 0, c), at(0, -1, 0, c), at(0, 0, 1, c), at(0, 0, -1, c)]
    peers += [at(1, 0, 0, c), at(-1, 0, 0, c), at(-1, 0, 1, c), at(1, 0, -1, c), at(0, 2, 0, c), at(0, -2, 0, c)]
    for peer in peers:
        pl.semaphore_signal(barrier, inc=1, device_id=peer, device_id_type=MESH)

    in_copies = [
        pltpu.make_async_copy(routes, rts, l_in.at[0]),
        pltpu.make_async_copy(gates, gts, l_in.at[1]),
        pltpu.make_async_copy(saved, sv, l_in.at[2]),
    ]
    for cp in in_copies:
        cp.start()
    w_copies = [
        pltpu.make_async_copy(w_down.at[:, pl.ds(k * CW, CW)], wv.at[pl.ds(k * width, width)], l_w.at[k])
        for k in range(nc)
    ]
    pl.semaphore_wait(barrier, len(peers))

    def send(src, dst, rsem, dev, k):
        pltpu.make_async_remote_copy(
            src_ref=src, dst_ref=dst, send_sem=s_tok.at[k], recv_sem=rsem,
            device_id=dev, device_id_type=MESH,
        ).start()

    def arrived(ref, rsem):
        pltpu.make_async_remote_copy(
            src_ref=ref, dst_ref=ref, send_sem=s_tok.at[0], recv_sem=rsem,
            device_id=at(0, 1, 0, c), device_id_type=MESH,
        ).wait_recv()

    def shard(k, b, yy):
        i = (c * 2 + b) * NY + yy
        return tok.at[k, pl.ds(pl.multiple_of(i * toks, toks), toks), :]

    def cols_of(k, core, b=None):
        m = NY if k == nc else col
        i = core * 2 if b is None else core * 2 + b
        rows = pl.ds(pl.multiple_of(i * m, m), m * (2 if b is None else 1))
        return meta.at[rows] if k == nc else tok.at[k, rows, :]

    def far(b, up):
        return 4 if (b == 0) == up else 3

    def y_send(k, b, up, d):
        step = 1 if up else -1
        ref = shard(k, b, (y - step * d + NY) % NY)
        send(ref, ref, r_y.at[k, b * 4 + d], at(0, step, 0, c), k)

    def y_arrived(k, b, d):
        arrived(tok.at[k, pl.ds(0, (2 if d < 4 else 1) * toks), :], r_y.at[k, b * 4 + d - 1])

    def first(k, b):
        arrived(shard(k, b, y), (r_z, r_x)[b].at[k])
        y_send(k, b, True, 0)
        y_send(k, b, False, 0)

    def hop(k, b, d):
        y_arrived(k, b, d)
        for up in (True, False):
            if d < far(b, up):
                y_send(k, b, up, d)

    def exchange(k, b):
        y_arrived(k, b, 4)
        ref = cols_of(k, c, b)
        send(ref, ref, r_d.at[k], at(0, 0, 0, 1 - c), k)

    def routing(step):
        def tile(dy):
            return meta.at[c * 2 * NY + (y + dy + NY) % NY]

        mine, before = cols_of(nc, c, 0), cols_of(nc, c, 1)
        if step == 1:
            for dy in (1, -1):
                send(tile(0), tile(0), r_m.at[0], at(0, dy, 0, c), nc)
        elif step == 2:
            arrived(meta.at[pl.ds(0, 2)], r_m.at[0])
            for dy, moved in ((3, (-1, 0, 1)), (-3, (-1, 0))):
                for j in moved:
                    send(tile(j), tile(j), r_m.at[1], at(0, dy, 0, c), nc)
        elif step == 3:
            arrived(meta.at[pl.ds(0, 5)], r_m.at[1])
            send(mine, before, r_m.at[2], at(0, 0, 1, c), nc)
            send(mine, mine, r_m.at[3], at(0, 0, 0, 1 - c), nc)
        else:
            arrived(before, r_m.at[2])
            send(before, before, r_m.at[3], at(0, 0, 0, 1 - c), nc)

    def build_tables():
        arrived(cols_of(nc, 1 - c), r_m.at[3])
        lane = lax.broadcasted_iota(I32, (8, 128), 1)
        group = lane // toks
        tables = []
        for cs in range(NCORE):
            for b in range(2):
                named = jnp.zeros((8, 128), F32)
                gate = jnp.zeros((8, 128), F32)
                for j in range(NY):
                    m = meta[(cs * 2 + b) * NY + j]
                    r = m if j == 0 else pltpu.roll(m, toks * j, 1)
                    shift = (toks * j - toks) % 128
                    g = m if shift == 0 else pltpu.roll(m, shift, 1)
                    named = jnp.where(group == j, r, named)
                    gate = jnp.where(group == j, g, gate)
                for xt in (x, (x - 1 + NX) % NX if b == 0 else (x + 1) % NX):
                    expert = ((y * NX + xt) * NCORE + c).astype(F32)
                    tables.append(jnp.sum(jnp.where(named == expert, gate, 0.0), axis=0, keepdims=True))
        assign = jnp.concatenate(tables, axis=0)
        live = jnp.where(assign > 0.0, 1.0, 0.0).astype(BF)
        from_ = lax.broadcasted_iota(I32, (128, 128), 0)
        to = lax.broadcasted_iota(I32, (128, 128), 1)
        tri = jnp.where((from_ // toks == to // toks) & (from_ < to), 1.0, 0.0).astype(BF)
        before = jnp.dot(live, tri, preferred_element_type=F32)
        before = jnp.where(assign > 0.0, before, -1.0)
        ri = lax.broadcasted_iota(I32, (n, 128), 0)
        li = lax.broadcasted_iota(I32, (n, 128), 1)
        same = (ri // MOST) == (li // toks)
        place = (ri % MOST).astype(F32)
        for cs in range(NCORE):
            for b in range(2):
                for t in range(2):
                    i = (cs * 2 + b) * 2 + t
                    r0 = (cs * 4 + t * 2 + b) * n
                    hit = same & (jnp.broadcast_to(before[i : i + 1], ri.shape) == place)
                    wt = jnp.where(hit, jnp.broadcast_to(assign[i : i + 1], ri.shape), 0.0)
                    pick[r0 : r0 + n, b * 128 : (b + 1) * 128] = jnp.where(hit, 1.0, 0.0).astype(BF)
                    pick[r0 : r0 + n, (1 - b) * 128 : (2 - b) * 128] = jnp.zeros((n, 128), BF)
                    weight[r0 : r0 + n, :] = jnp.broadcast_to(jnp.sum(wt, axis=1, keepdims=True), (n, 128))

    def build_perm():
        slot = lax.broadcasted_iota(I32, (256, 256), 0)
        place = lax.broadcasted_iota(I32, (256, 256), 1)
        ys, xs, cs, p = slot // 32, (slot // 8) % NX, (slot // 4) % NCORE, slot % MOST
        dx = (xs - x + NX) % NX
        rel = jnp.where(dx == 0, 0, jnp.where(dx == 3, 1, jnp.where(dx == 1, 2, 3)))
        perm[...] = jnp.where(place == rel * 64 + cs * 32 + ys * 4 + p, 1.0, 0.0).astype(BF)

    def factors(q):
        m = sv.shape[0] // 4
        sl = slice(q * m, (q + 1) * m)
        pre_gate = sv[sl, :width].astype(F32)
        pre_up = sv[sl, width:].astype(F32)
        sig = jax.nn.sigmoid(pre_gate)
        ufac[sl, :] = pre_gate * sig
        gfac[sl, :] = pre_up * sig * (1.0 + pre_gate * (1.0 - sig))

    def select(k):
        arrived(cols_of(k, 1 - c), r_d.at[k])
        for cs in range(NCORE):
            res = jnp.dot(pick[cs * 128 : (cs + 1) * 128, :], tok[k, cs * 2 * col : (cs + 1) * 2 * col, :],
                          preferred_element_type=F32)
            wt = weight[cs * 128 : (cs + 1) * 128, :]
            rows = jnp.concatenate([res[:, i * 128 : (i + 1) * 128] * wt for i in range(CW // 128)], axis=1).astype(BF)
            snd[k, 0, cs] = rows[2 * n : 3 * n]
            snd[k, 1, cs] = rows[3 * n : 4 * n]
            row[k, 0, cs] = rows[0:n]
            row[k, 1, cs] = rows[n : 2 * n]
        send(snd.at[k, 0], row.at[k, 2], r_r.at[k], at(0, 0, -1, c), k)
        send(snd.at[k, 1], row.at[k, 3], r_r.at[k], at(0, 0, 1, c), k)

    def main(k):
        arrived(row.at[k, 2:4], r_r.at[k])
        w_copies[k].wait()
        lhs = jnp.dot(perm[...], row[k].reshape(256, CW), preferred_element_type=F32).astype(BF)
        for i in range(4):
            cols = slice(i * ncols, (i + 1) * ncols)
            wk = wv[k * width + i * ncols : k * width + (i + 1) * ncols, :]
            part = lax.dot_general(lhs, wk, (((1,), (1,)), ((), ())), preferred_element_type=F32)
            if k > 0:
                part = acc[:, cols] + part
            if k < nc - 1:
                acc[:, cols] = part
            else:
                out[:, cols] = (part * gfac[:, cols]).astype(BF)
                out[:, width + i * ncols : width + (i + 1) * ncols] = (part * ufac[:, cols]).astype(BF)

    for k in range(nc):
        part = grad.at[:, pl.ds(k * CW, CW)]
        send(part, shard(k, 0, y), r_z.at[k], at(-1, 0, 0, c), k)
        send(part, shard(k, 1, y), r_x.at[k], at(-1, 0, 1, c), k)
    for cp in w_copies:
        cp.start()
    in_copies[0].wait()
    in_copies[1].wait()
    own = (c * 2) * NY + y
    meta[own, :, 0:toks] = rts[...].astype(F32)
    meta[own, :, toks : 2 * toks] = gts[...]
    routing(1)
    build_perm()
    in_copies[2].wait()
    for q in range(4):
        factors(q)

    for kind, k, b, d in ORDER:
        with jax.named_scope(f"{'fhesmq'[kind]}{b}{d}_{k}"):
            if kind == 0:
                first(k, b)
            elif kind == 1:
                hop(k, b, d)
            elif kind == 2:
                exchange(k, b)
            elif kind == 3:
                build_tables() if k == nc else select(k)
            elif kind == 4:
                main(k)
            else:
                routing(d)

    for k in range(nc):
        ref = wv.at[pl.ds(0, 16 * toks + 2 * col + 4 * n)]
        pltpu.make_async_copy(ref, ref, s_tok.at[k]).wait()
    ref = meta.at[pl.ds(0, 15 + 2 * NY)]
    pltpu.make_async_copy(ref, ref, s_tok.at[nc]).wait()


def per_device(sections, next_grad, routes, gates, saved, w_down):
    toks, d = next_grad.shape[1:]
    slots, width2 = saved.shape[2:]
    width = width2 // 2
    nc = d // CW
    dma = pltpu.SemaphoreType.DMA
    args = (next_grad[0], routes[0].T, gates[0].T, saved[0, 0], w_down[0])
    res = pl.pallas_call(
        functools.partial(kernel, sections, nc),
        out_shape=jax.ShapeDtypeStruct((slots, width2), BF),
        in_specs=[pl.BlockSpec(memory_space=pltpu.HBM)] * 5,
        out_specs=pl.BlockSpec(memory_space=pltpu.VMEM),
        scratch_shapes=[
            pltpu.VMEM((nc, NCORE * 2 * NY * toks, CW), BF),
            pltpu.VMEM((nc, 4, NCORE, NY * MOST, CW), BF),
            pltpu.VMEM((nc, 2, NCORE, NY * MOST, CW), BF),
            pltpu.VMEM((nc * width, CW), BF),
            pltpu.VMEM((slots, width2), BF),
            pltpu.VMEM((slots, width), F32),
            pltpu.VMEM((slots, width), F32),
            pltpu.VMEM((slots, width), F32),
            pltpu.VMEM(routes.shape[:0:-1], I32),
            pltpu.VMEM(gates.shape[:0:-1], F32),
            pltpu.VMEM((NCORE * 2 * NY, 8, 128), F32),
            pltpu.VMEM((256, 256), BF),
            pltpu.VMEM((256, 128), F32),
            pltpu.VMEM((256, 256), BF),
            dma((nc, 8)),
            dma((nc,)),
            dma((nc,)),
            dma((nc,)),
            dma((nc,)),
            dma((4,)),
            dma((nc + 1,)),
            dma((3,)),
            dma((nc,)),
        ],
        compiler_params=pltpu.CompilerParams(collective_id=0, has_side_effects=True, vmem_limit_bytes=40 << 20),
    )(*[pltpu.with_memory_space_constraint(v, pltpu.HBM) for v in args])
    return res[None, None]


def solution(mesh):
    return jax.shard_map(
        functools.partial(per_device, mesh.shape["section"]),
        mesh=mesh,
        in_specs=(
            P("section", "expert", None),
            P("section", "expert", None),
            P("section", "expert", None),
            P("section", "expert", None, None),
            P("expert", None, None),
        ),
        out_specs=P("section", "expert", None, None),
        check_vma=False,
    )
```

time: 93.3 us -> 55.1 us (0.59)
  Pallas kernels: 0 us -> 54 us
  waiting for transfers between devices: 44.4 us -> 0 us
  starting transfers between devices: 30.2 us -> 0 us
  matrix products: 6.94 us -> 0 us
  local copies, waits for them, and re-layouts: 6.71 us -> 0.97 us
  other arithmetic: 4.45 us -> 0 us
    pallas_call x0 -> x1, Pallas kernels: none -> 54 us  [per_device(): pl.pallas_call(functools.partial(kernel, sections, nc), out_shape=jax.Sha...]
    all_to_all x1 -> x0, waiting for transfers between devices: 44.4 us -> none  [dispatch(): lax.all_to_all(rows, 'expert', split_axis=0, concat_axis=0, tiled=True)]
    ppermute x1 -> x0, starting transfers between devices: 18.7 us -> none  [passed_along(): return lax.ppermute(x, axis, [(i, (i + by) % peers) for i in range(peers)])]
    all_to_all x1 -> x0, starting transfers between devices: 11.4 us -> none  [dispatch(): lax.all_to_all(rows, 'expert', split_axis=0, concat_axis=0, tiled=True)]
    dot_general x1 -> x0, matrix products: 6.94 us -> none  [per_device(): lax.dot_general(received, w_down[0], (((1,), (1,)), ((), ())), preferred_...]
    convert_element_type x1 -> x0, other arithmetic: 4.19 us -> none  [build_rows(): return rows.astype(jnp.bfloat16).reshape(pick.shape[1], most, grad.shape[1])]
    gather x2 -> x0, local copies, waits for them, and re-layouts: 3.2 us -> none  [build_rows(): taken = jnp.take(grad, flat_ids, axis=0).astype(jnp.float32)]
    reshape x2 -> x0, local copies, waits for them, and re-layouts: 1.57 us -> none  [the longest x1 1.46 us: per_device(): received = received.reshape(slots, received.shape[2])]
  transfers between devices with their start and end apart: 2 -> 0, of which waited for: 1 -> 0; matrix products, arithmetic and copies ran while one was open for 2% -> 0% of each run, Pallas kernels for 0% -> 0%
where the time goes in v2:
time: 55.1 us; the launch traced here: 55 us
  Pallas kernels  54 us (98%)
  local copies, waits for them, and re-layouts  0.97 us (2%)
    pallas_call x1, Pallas kernels, per_device(): pl.pallas_call(functools.partial(kernel, sections, nc), out_shape=jax.Sha...  54 us

profile of v2, /device:TPU:1, one launch (start us, length us, event | category | flops | bytes accessed | tf_op | source)
XLA Modules:
  0.0 55.0 jit_solution(6121629681290767020)
XLA Ops:
  0.0 54.0 %shard_map.55 = bf16[256,2048]{1,0:T(8,128)(2,1)S(1)} custom-call(bf16[16,3584]{1,0:T(8,128)(2,1)} %bitcast.13, s32[8,16]{1,0:T(8,128)} %bitcast.14, f32[8,16]{1,0:T(8,128)} %bitcast.15, bf16[256,2048]{1,0:T(8,128)(2,1)} %bitcast.12, bf16[1024,3584]{1,0:T(8,128)(2,1)} %bitcast.11), custom_call_target="tpu_custom_call" | custom-call | tf_op jit(solution)/shard_map/pallas_call | solution.py:270
  54.0 1.0 %copy.7 = bf16[1,1,256,2048]{3,2,1,0:T(8,128)(2,1)} copy(bf16[1,1,256,2048]{3,2,1,0:T(8,128)(2,1)S(1)} %bitcast.10) | data formatting | bytes 2097152

commit v3 on v2

--- a/solution.py
+++ b/solution.py
@@ -14,17 +14,20 @@
 BF, F32, I32 = jnp.bfloat16, jnp.float32, jnp.int32
 
 ORDER = (
-    (0, 0, 0, 0), (0, 0, 1, 0), (0, 1, 0, 0), (5, 7, 0, 2), (0, 1, 1, 0), (0, 2, 0, 0), (0, 2, 1, 0), (0, 3, 0, 0),
-    (0, 3, 1, 0), (0, 4, 0, 0), (1, 0, 0, 1), (0, 4, 1, 0), (0, 5, 0, 0), (1, 0, 1, 1), (1, 1, 0, 1), (0, 5, 1, 0),
-    (0, 6, 0, 0), (1, 1, 1, 1), (1, 2, 0, 1), (1, 2, 1, 1), (5, 7, 0, 3), (1, 3, 0, 1), (1, 3, 1, 1), (1, 4, 0, 1),
-    (1, 0, 0, 2), (1, 4, 1, 1), (1, 5, 0, 1), (1, 0, 1, 2), (1, 1, 0, 2), (0, 6, 1, 0), (5, 7, 0, 4), (1, 5, 1, 1),
-    (1, 1, 1, 2), (1, 2, 0, 2), (1, 2, 1, 2), (1, 3, 0, 2), (1, 3, 1, 2), (3, 7, 0, 0), (1, 0, 0, 3), (1, 4, 0, 2),
-    (1, 4, 1, 2), (1, 6, 0, 1), (1, 0, 1, 3), (1, 5, 0, 2), (1, 1, 0, 3), (1, 6, 1, 1), (1, 5, 1, 2), (1, 1, 1, 3),
-    (1, 2, 0, 3), (1, 2, 1, 3), (1, 3, 0, 3), (1, 3, 1, 3), (2, 0, 0, 0), (1, 4, 0, 3), (1, 4, 1, 3), (2, 0, 1, 0),
-    (1, 6, 0, 2), (1, 5, 0, 3), (2, 1, 0, 0), (1, 6, 1, 2), (2, 1, 1, 0), (1, 5, 1, 3), (2, 2, 1, 0), (2, 2, 0, 0),
-    (2, 3, 1, 0), (3, 0, 0, 0), (2, 3, 0, 0), (2, 4, 0, 0), (2, 4, 1, 0), (1, 6, 0, 3), (2, 5, 0, 0), (3, 1, 0, 0),
-    (1, 6, 1, 3), (3, 2, 0, 0), (2, 5, 1, 0), (3, 3, 0, 0), (3, 4, 0, 0), (2, 6, 0, 0), (3, 5, 0, 0), (2, 6, 1, 0),
-    (4, 0, 0, 0), (4, 1, 0, 0), (3, 6, 0, 0), (4, 2, 0, 0), (4, 3, 0, 0), (4, 4, 0, 0), (4, 5, 0, 0), (4, 6, 0, 0),
+    (0, 0, 0, 0), (0, 0, 1, 0), (5, 7, 0, 2), (0, 1, 0, 0), (0, 1, 1, 0), (0, 2, 0, 0), (0, 2, 1, 0), (0, 3, 0, 0),
+    (0, 3, 1, 0), (0, 4, 0, 0), (1, 0, 0, 1), (0, 4, 1, 0), (0, 5, 0, 0), (1, 0, 1, 1), (0, 5, 1, 0), (0, 6, 0, 0),
+    (1, 1, 0, 1), (0, 6, 1, 0), (1, 1, 1, 1), (1, 2, 0, 1), (5, 7, 0, 3), (1, 2, 1, 1), (1, 3, 0, 1), (1, 3, 1, 1),
+    (1, 4, 0, 1), (1, 0, 0, 2), (2, 0, 0, 0), (1, 4, 1, 1), (1, 5, 0, 1), (1, 0, 1, 2), (2, 0, 1, 0), (1, 5, 1, 1),
+    (1, 6, 0, 1), (1, 1, 0, 2), (5, 7, 0, 4), (2, 1, 0, 0), (1, 6, 1, 1), (1, 1, 1, 2), (2, 1, 1, 0), (1, 2, 0, 2),
+    (3, 7, 0, 0), (3, 0, 0, 0), (3, 1, 0, 0), (2, 2, 0, 0), (1, 2, 1, 2), (2, 2, 1, 0), (1, 3, 0, 2), (2, 3, 0, 0),
+    (1, 3, 1, 2), (2, 3, 1, 0), (1, 4, 0, 2), (2, 4, 0, 0), (1, 0, 0, 3), (1, 4, 1, 2), (3, 2, 0, 0), (3, 3, 0, 0),
+    (2, 4, 1, 0), (1, 0, 1, 3), (1, 5, 0, 2), (2, 5, 0, 0), (1, 5, 1, 2), (2, 5, 1, 0), (1, 6, 0, 2), (3, 4, 0, 0),
+    (3, 5, 0, 0), (1, 1, 0, 3), (1, 1, 1, 3), (2, 6, 0, 0), (1, 6, 1, 2), (2, 6, 1, 0), (1, 2, 0, 3), (1, 2, 1, 3),
+    (1, 3, 0, 3), (3, 6, 0, 0), (1, 3, 1, 3), (1, 4, 0, 3), (2, 0, 0, 1), (2, 0, 1, 1), (1, 4, 1, 3), (1, 5, 0, 3),
+    (1, 5, 1, 3), (3, 0, 0, 1), (2, 1, 0, 1), (2, 1, 1, 1), (1, 6, 0, 3), (1, 6, 1, 3), (2, 2, 1, 1), (2, 2, 0, 1),
+    (2, 3, 1, 1), (3, 1, 0, 1), (2, 3, 0, 1), (2, 4, 0, 1), (3, 2, 0, 1), (2, 4, 1, 1), (2, 5, 0, 1), (3, 3, 0, 1),
+    (2, 5, 1, 1), (3, 4, 0, 1), (2, 6, 0, 1), (2, 6, 1, 1), (3, 5, 0, 1), (4, 0, 0, 0), (3, 6, 0, 1), (4, 1, 0, 0),
+    (4, 2, 0, 0), (4, 3, 0, 0), (4, 4, 0, 0), (4, 5, 0, 0), (4, 6, 0, 0),
 )
 
 
@@ -37,7 +40,8 @@
     width = w_down.shape[0]
     ncols = width // 4
     n = NY * MOST
-    col = NY * toks
+    half = NY * toks // 2
+    m16 = n // 2
 
     def at(ds, dy, dx, core):
         ss = (s + ds + sections) % sections
@@ -75,29 +79,23 @@
             device_id=at(0, 1, 0, c), device_id_type=MESH,
         ).wait_recv()
 
-    def shard(k, b, yy):
-        i = (c * 2 + b) * NY + yy
-        return tok.at[k, pl.ds(pl.multiple_of(i * toks, toks), toks), :]
-
-    def cols_of(k, core, b=None):
-        m = NY if k == nc else col
-        i = core * 2 if b is None else core * 2 + b
-        rows = pl.ds(pl.multiple_of(i * m, m), m * (2 if b is None else 1))
-        return meta.at[rows] if k == nc else tok.at[k, rows, :]
+    def shard(k, b, dy):
+        j = (dy + 2) % NY
+        rows = pl.multiple_of((c * 2 + b) * half + (j % (NY // 2)) * toks, toks)
+        return tok.at[k, j // (NY // 2), pl.ds(rows, toks), :]
 
     def far(b, up):
         return 4 if (b == 0) == up else 3
 
     def y_send(k, b, up, d):
         step = 1 if up else -1
-        ref = shard(k, b, (y - step * d + NY) % NY)
-        send(ref, ref, r_y.at[k, b * 4 + d], at(0, step, 0, c), k)
+        send(shard(k, b, -step * d), shard(k, b, -step * (d + 1)), r_y.at[k, b * 4 + d], at(0, step, 0, c), k)
 
     def y_arrived(k, b, d):
-        arrived(tok.at[k, pl.ds(0, (2 if d < 4 else 1) * toks), :], r_y.at[k, b * 4 + d - 1])
+        arrived(tok.at[k, 0, pl.ds(0, (2 if d < 4 else 1) * toks), :], r_y.at[k, b * 4 + d - 1])
 
     def first(k, b):
-        arrived(shard(k, b, y), (r_z, r_x)[b].at[k])
+        arrived(shard(k, b, 0), (r_z, r_x)[b].at[k])
         y_send(k, b, True, 0)
         y_send(k, b, False, 0)
 
@@ -107,16 +105,17 @@
             if d < far(b, up):
                 y_send(k, b, up, d)
 
-    def exchange(k, b):
-        y_arrived(k, b, 4)
-        ref = cols_of(k, c, b)
-        send(ref, ref, r_d.at[k], at(0, 0, 0, 1 - c), k)
+    def exchange(k, b, p):
+        if p == 1:
+            y_arrived(k, b, 4)
+        ref = tok.at[k, p, pl.ds(pl.multiple_of((c * 2 + b) * half, half), half), :]
+        send(ref, ref, r_d.at[k, p], at(0, 0, 0, 1 - c), k)
 
     def routing(step):
         def tile(dy):
             return meta.at[c * 2 * NY + (y + dy + NY) % NY]
 
-        mine, before = cols_of(nc, c, 0), cols_of(nc, c, 1)
+        mine, before = [meta.at[pl.ds(pl.multiple_of((c * 2 + b) * NY, NY), NY)] for b in range(2)]
         if step == 1:
             for dy in (1, -1):
                 send(tile(0), tile(0), r_m.at[0], at(0, dy, 0, c), nc)
@@ -134,7 +133,7 @@
             send(before, before, r_m.at[3], at(0, 0, 0, 1 - c), nc)
 
     def build_tables():
-        arrived(cols_of(nc, 1 - c), r_m.at[3])
+        arrived(meta.at[pl.ds(0, 2 * NY)], r_m.at[3])
         lane = lax.broadcasted_iota(I32, (8, 128), 1)
         group = lane // toks
         tables = []
@@ -143,7 +142,7 @@
                 named = jnp.zeros((8, 128), F32)
                 gate = jnp.zeros((8, 128), F32)
                 for j in range(NY):
-                    m = meta[(cs * 2 + b) * NY + j]
+                    m = meta[(cs * 2 + b) * NY + (y + j - 2 + NY) % NY]
                     r = m if j == 0 else pltpu.roll(m, toks * j, 1)
                     shift = (toks * j - toks) % 128
                     g = m if shift == 0 else pltpu.roll(m, shift, 1)
@@ -159,20 +158,25 @@
         tri = jnp.where((from_ // toks == to // toks) & (from_ < to), 1.0, 0.0).astype(BF)
         before = jnp.dot(live, tri, preferred_element_type=F32)
         before = jnp.where(assign > 0.0, before, -1.0)
-        ri = lax.broadcasted_iota(I32, (n, 128), 0)
-        li = lax.broadcasted_iota(I32, (n, 128), 1)
-        same = (ri // MOST) == (li // toks)
+        turned = [(assign, before), (pltpu.roll(assign, half, 1), pltpu.roll(before, half, 1))]
+        ri = lax.broadcasted_iota(I32, (m16, 128), 0)
+        li = lax.broadcasted_iota(I32, (m16, 128), 1)
+        same = (ri // MOST) == (li % half) // toks
         place = (ri % MOST).astype(F32)
-        for cs in range(NCORE):
-            for b in range(2):
-                for t in range(2):
-                    i = (cs * 2 + b) * 2 + t
-                    r0 = (cs * 4 + t * 2 + b) * n
-                    hit = same & (jnp.broadcast_to(before[i : i + 1], ri.shape) == place)
-                    wt = jnp.where(hit, jnp.broadcast_to(assign[i : i + 1], ri.shape), 0.0)
-                    pick[r0 : r0 + n, b * 128 : (b + 1) * 128] = jnp.where(hit, 1.0, 0.0).astype(BF)
-                    pick[r0 : r0 + n, (1 - b) * 128 : (2 - b) * 128] = jnp.zeros((n, 128), BF)
-                    weight[r0 : r0 + n, :] = jnp.broadcast_to(jnp.sum(wt, axis=1, keepdims=True), (n, 128))
+        for p in range(2):
+            for cs in range(NCORE):
+                for b in range(2):
+                    gates_, places_ = turned[0 if b == p else 1]
+                    here = same & (li // half == b)
+                    for t in range(2):
+                        i = (cs * 2 + b) * 2 + t
+                        r0 = (t * 4 + b * 2 + cs) * m16
+                        hit = here & (jnp.broadcast_to(places_[i : i + 1], ri.shape) == place)
+                        wt = jnp.where(hit, jnp.broadcast_to(gates_[i : i + 1], ri.shape), 0.0)
+                        rows = slice(r0, r0 + m16)
+                        pick[p, rows, cs * 128 : (cs + 1) * 128] = jnp.where(hit, 1.0, 0.0).astype(BF)
+                        pick[p, rows, (1 - cs) * 128 : (2 - cs) * 128] = jnp.zeros((m16, 128), BF)
+                        weight[p, rows, :] = jnp.broadcast_to(jnp.sum(wt, axis=1, keepdims=True), (m16, 128))
 
     def build_perm():
         slot = lax.broadcasted_iota(I32, (256, 256), 0)
@@ -180,7 +184,9 @@
         ys, xs, cs, p = slot // 32, (slot // 8) % NX, (slot // 4) % NCORE, slot % MOST
         dx = (xs - x + NX) % NX
         rel = jnp.where(dx == 0, 0, jnp.where(dx == 3, 1, jnp.where(dx == 1, 2, 3)))
-        perm[...] = jnp.where(place == rel * 64 + cs * 32 + ys * 4 + p, 1.0, 0.0).astype(BF)
+        j = (ys - y + 2 + NY) % NY
+        spot = (j // 4) * 128 + rel * 32 + cs * 16 + (j % 4) * MOST + p
+        perm[...] = jnp.where(place == spot, 1.0, 0.0).astype(BF)
 
     def factors(q):
         m = sv.shape[0] // 4
@@ -191,22 +197,20 @@
         ufac[sl, :] = pre_gate * sig
         gfac[sl, :] = pre_up * sig * (1.0 + pre_gate * (1.0 - sig))
 
-    def select(k):
-        arrived(cols_of(k, 1 - c), r_d.at[k])
-        for cs in range(NCORE):
-            res = jnp.dot(pick[cs * 128 : (cs + 1) * 128, :], tok[k, cs * 2 * col : (cs + 1) * 2 * col, :],
-                          preferred_element_type=F32)
-            wt = weight[cs * 128 : (cs + 1) * 128, :]
-            rows = jnp.concatenate([res[:, i * 128 : (i + 1) * 128] * wt for i in range(CW // 128)], axis=1).astype(BF)
-            snd[k, 0, cs] = rows[2 * n : 3 * n]
-            snd[k, 1, cs] = rows[3 * n : 4 * n]
-            row[k, 0, cs] = rows[0:n]
-            row[k, 1, cs] = rows[n : 2 * n]
-        send(snd.at[k, 0], row.at[k, 2], r_r.at[k], at(0, 0, -1, c), k)
-        send(snd.at[k, 1], row.at[k, 3], r_r.at[k], at(0, 0, 1, c), k)
+    def select(k, p):
+        arrived(tok.at[k, p, pl.ds(0, 2 * half), :], r_d.at[k, p])
+        res = jnp.dot(pick[p], tok[k, p], preferred_element_type=F32)
+        wt = weight[p]
+        rows = jnp.concatenate([res[:, i * 128 : (i + 1) * 128] * wt for i in range(CW // 128)], axis=1).astype(BF)
+        snd[k, p, 0] = rows[2 * n : 3 * n]
+        snd[k, p, 1] = rows[3 * n : 4 * n]
+        row[k, p, 0] = rows[0:n]
+        row[k, p, 1] = rows[n : 2 * n]
+        send(snd.at[k, p, 0], row.at[k, p, 2], r_r.at[k], at(0, 0, -1, c), k)
+        send(snd.at[k, p, 1], row.at[k, p, 3], r_r.at[k], at(0, 0, 1, c), k)
 
     def main(k):
-        arrived(row.at[k, 2:4], r_r.at[k])
+        arrived(wv.at[pl.ds(0, 4 * n)], r_r.at[k])
         w_copies[k].wait()
         lhs = jnp.dot(perm[...], row[k].reshape(256, CW), preferred_element_type=F32).astype(BF)
         for i in range(4):
@@ -223,8 +227,8 @@
 
     for k in range(nc):
         part = grad.at[:, pl.ds(k * CW, CW)]
-        send(part, shard(k, 0, y), r_z.at[k], at(-1, 0, 0, c), k)
-        send(part, shard(k, 1, y), r_x.at[k], at(-1, 0, 1, c), k)
+        send(part, shard(k, 0, 0), r_z.at[k], at(-1, 0, 0, c), k)
+        send(part, shard(k, 1, 0), r_x.at[k], at(-1, 0, 1, c), k)
     for cp in w_copies:
         cp.start()
     in_copies[0].wait()
@@ -245,16 +249,16 @@
             elif kind == 1:
                 hop(k, b, d)
             elif kind == 2:
-                exchange(k, b)
+                exchange(k, b, d)
             elif kind == 3:
-                build_tables() if k == nc else select(k)
+                build_tables() if k == nc else select(k, d)
             elif kind == 4:
                 main(k)
             else:
                 routing(d)
 
     for k in range(nc):
-        ref = wv.at[pl.ds(0, 16 * toks + 2 * col + 4 * n)]
+        ref = wv.at[pl.ds(0, 16 * toks + 4 * half + 4 * n)]
         pltpu.make_async_copy(ref, ref, s_tok.at[k]).wait()
     ref = meta.at[pl.ds(0, 15 + 2 * NY)]
     pltpu.make_async_copy(ref, ref, s_tok.at[nc]).wait()
@@ -273,9 +277,9 @@
         in_specs=[pl.BlockSpec(memory_space=pltpu.HBM)] * 5,
         out_specs=pl.BlockSpec(memory_space=pltpu.VMEM),
         scratch_shapes=[
-            pltpu.VMEM((nc, NCORE * 2 * NY * toks, CW), BF),
-            pltpu.VMEM((nc, 4, NCORE, NY * MOST, CW), BF),
-            pltpu.VMEM((nc, 2, NCORE, NY * MOST, CW), BF),
+            pltpu.VMEM((nc, 2, NCORE * NY * toks, CW), BF),
+            pltpu.VMEM((nc, 2, 4, NY * MOST, CW), BF),
+            pltpu.VMEM((nc, 2, 2, NY * MOST, CW), BF),
             pltpu.VMEM((nc * width, CW), BF),
             pltpu.VMEM((slots, width2), BF),
             pltpu.VMEM((slots, width), F32),
@@ -284,13 +288,13 @@
             pltpu.VMEM(routes.shape[:0:-1], I32),
             pltpu.VMEM(gates.shape[:0:-1], F32),
             pltpu.VMEM((NCORE * 2 * NY, 8, 128), F32),
-            pltpu.VMEM((256, 256), BF),
-            pltpu.VMEM((256, 128), F32),
+            pltpu.VMEM((2, 128, 256), BF),
+            pltpu.VMEM((2, 128, 128), F32),
             pltpu.VMEM((256, 256), BF),
             dma((nc, 8)),
             dma((nc,)),
             dma((nc,)),
-            dma((nc,)),
+            dma((nc, 2)),
             dma((nc,)),
             dma((4,)),
             dma((nc + 1,)),

time: 55.1 us -> 52 us (0.944)
  Pallas kernels: 54 us -> 50.9 us
    pallas_call x1, Pallas kernels: 54 us -> 50.9 us  [per_device(): pl.pallas_call(functools.partial(kernel, sections, nc), out_shape=jax.Sha...]
where the time goes in v3:
time: 52 us; the launch traced here: 51.9 us
  Pallas kernels  50.9 us (98%)
  local copies, waits for them, and re-layouts  0.97 us (2%)
    pallas_call x1, Pallas kernels, per_device(): pl.pallas_call(functools.partial(kernel, sections, nc), out_shape=jax.Sha...  50.9 us

profile of v3, /device:TPU:1, one launch (start us, length us, event | category | flops | bytes accessed | tf_op | source)
XLA Modules:
  0.0 51.9 jit_solution(7579859503022037430)
XLA Ops:
  0.0 50.9 %shard_map.55 = bf16[256,2048]{1,0:T(8,128)(2,1)S(1)} custom-call(bf16[16,3584]{1,0:T(8,128)(2,1)} %bitcast.13, s32[8,16]{1,0:T(8,128)} %bitcast.14, f32[8,16]{1,0:T(8,128)} %bitcast.15, bf16[256,2048]{1,0:T(8,128)(2,1)} %bitcast.12, bf16[1024,3584]{1,0:T(8,128)(2,1)} %bitcast.11), custom_call_target="tpu_custom_call" | custom-call | tf_op jit(solution)/shard_map/pallas_call | solution.py:274
  50.9 1.0 %copy.7 = bf16[1,1,256,2048]{3,2,1,0:T(8,128)(2,1)} copy(bf16[1,1,256,2048]{3,2,1,0:T(8,128)(2,1)S(1)} %bitcast.10) | data formatting | bytes 2097152

commit v4 on v3

--- a/solution.py
+++ b/solution.py
@@ -62,7 +62,7 @@
     for cp in in_copies:
         cp.start()
     w_copies = [
-        pltpu.make_async_copy(w_down.at[:, pl.ds(k * CW, CW)], wv.at[pl.ds(k * width, width)], l_w.at[k])
+        pltpu.make_async_copy(w_down.at[:, pl.ds(k * CW, CW)], wv.at[pl.ds(k * width, width)], l_w)
         for k in range(nc)
     ]
     pl.semaphore_wait(barrier, len(peers))
@@ -211,7 +211,8 @@
 
     def main(k):
         arrived(wv.at[pl.ds(0, 4 * n)], r_r.at[k])
-        w_copies[k].wait()
+        if k == 0:
+            pltpu.make_async_copy(wv, wv, l_w).wait()
         lhs = jnp.dot(perm[...], row[k].reshape(256, CW), preferred_element_type=F32).astype(BF)
         for i in range(4):
             cols = slice(i * ncols, (i + 1) * ncols)
@@ -299,7 +300,7 @@
             dma((4,)),
             dma((nc + 1,)),
             dma((3,)),
-            dma((nc,)),
+            dma,
         ],
         compiler_params=pltpu.CompilerParams(collective_id=0, has_side_effects=True, vmem_limit_bytes=40 << 20),
     )(*[pltpu.with_memory_space_constraint(v, pltpu.HBM) for v in args])

time: 52 us -> 51.9 us (level)
  no operation moved by 1% of the time
where the time goes in v4:
time: 51.9 us; the launch traced here: 51.8 us
  Pallas kernels  50.8 us (98%)
  local copies, waits for them, and re-layouts  0.97 us (2%)
    pallas_call x1, Pallas kernels, per_device(): pl.pallas_call(functools.partial(kernel, sections, nc), out_shape=jax.Sha...  50.8 us

profile of v4, /device:TPU:1, one launch (start us, length us, event | category | flops | bytes accessed | tf_op | source)
XLA Modules:
  0.0 51.8 jit_solution(17942038691697647800)
XLA Ops:
  0.0 50.8 %shard_map.55 = bf16[256,2048]{1,0:T(8,128)(2,1)S(1)} custom-call(bf16[16,3584]{1,0:T(8,128)(2,1)} %bitcast.13, s32[8,16]{1,0:T(8,128)} %bitcast.14, f32[8,16]{1,0:T(8,128)} %bitcast.15, bf16[256,2048]{1,0:T(8,128)(2,1)} %bitcast.12, bf16[1024,3584]{1,0:T(8,128)(2,1)} %bitcast.11), custom_call_target="tpu_custom_call" | custom-call | tf_op jit(solution)/shard_map/pallas_call | solution.py:275
  50.8 1.0 %copy.7 = bf16[1,1,256,2048]{3,2,1,0:T(8,128)(2,1)} copy(bf16[1,1,256,2048]{3,2,1,0:T(8,128)(2,1)S(1)} %bitcast.10) | data formatting | bytes 2097152
